TPU v7x, 128 devices: a whole 4x4x4 slice. The times are simulated.
128 devices in a mesh: fsdp: 16 (over x_lo, y, core), tp: 8 (over x_hi, z).
Axes of the slice: x: 4 (x_hi: 2, x_lo: 2; x = x_hi * 2 + x_lo), y: 4, z: 4, core: 2. Of those that a mesh axis runs over, the one named last changes fastest.
Arguments:
- tokens: bfloat16 [16384, 2048], P(('fsdp', 'tp')), may hold values from -6 to 6
- grad_out: bfloat16 [16384, 2048], P(('fsdp', 'tp')), may hold values from -6 to 6
- adapter_ids: int32 [16], P('fsdp'), may hold values from 0 to 7
- first_gain: float32 [2048], replicated, may hold values from 0.1 to 1.9
- first_shift: float32 [2048], replicated, may hold values from -4 to 4
- joined_weight: bfloat16 [2048, 6144], P('fsdp', 'tp'), may hold values from -0.125 to 0.125
- joined_bias: float32 [6144], P('tp'), may hold values from -4 to 4
- dense_weight: bfloat16 [2048, 2048], P('tp', 'fsdp'), may hold values from -0.5 to 0.5
- dense_bias: float32 [2048], replicated, may hold values from -4 to 4
- second_gain: float32 [2048], replicated, may hold values from 0.1 to 1.9
- second_shift: float32 [2048], replicated, may hold values from -4 to 4
- up_weight: bfloat16 [2048, 8192], P('fsdp', 'tp'), may hold values from -0.125 to 0.125
- up_bias: float32 [8192], P('tp'), may hold values from -6 to 6
- down_weight: bfloat16 [8192, 2048], P('tp', 'fsdp'), may hold values from -0.125 to 0.125
- down_bias: float32 [2048], replicated, may hold values from -4 to 4
- joined_adapt_in: bfloat16 [8, 2048, 16], replicated, may hold values from -0.125 to 0.125
- joined_adapt_out: bfloat16 [8, 16, 6144], P(None, None, 'tp'), may hold values from -2 to 2
- dense_adapt_in: bfloat16 [8, 2048, 16], P(None, 'tp'), may hold values from -0.5 to 0.5
- dense_adapt_out: bfloat16 [8, 16, 2048], replicated, may hold values from -2 to 2
- up_adapt_in: bfloat16 [8, 2048, 16], replicated, may hold values from -0.125 to 0.125
- up_adapt_out: bfloat16 [8, 16, 8192], P(None, None, 'tp'), may hold values from -2 to 2
- down_adapt_in: bfloat16 [8, 8192, 16], P(None, 'tp'), may hold values from -0.125 to 0.125
- down_adapt_out: bfloat16 [8, 16, 2048], replicated, may hold values from -2 to 2
Outputs:
- layer_out: bfloat16 [16384, 2048], P(('fsdp', 'tp'))
- grad_tokens: float32 [16384, 2048], P(('fsdp', 'tp'))
- grad_joined_in: float32 [8, 2048, 16], replicated
- grad_joined_out: float32 [8, 16, 6144], P(None, None, 'tp')
- grad_dense_in: float32 [8, 2048, 16], P(None, 'tp')
- grad_dense_out: float32 [8, 16, 2048], replicated
- grad_up_in: float32 [8, 2048, 16], replicated
- grad_up_out: float32 [8, 16, 8192], P(None, None, 'tp')
- grad_down_in: float32 [8, 8192, 16], P(None, 'tp')
- grad_down_out: float32 [8, 16, 2048], replicated
All inputs are finite; a program needn't handle non-finite values.
Results may differ from a plain program's by a relative error of at most 0.02.
Values may be sent and summed in bfloat16 or wider, within the bound.
A program may use at most 128 MiB of HBM per device.

v0:
```python
import jax
import jax.numpy as jnp
from jax import lax
from jax.sharding import PartitionSpec as P

HEADS = 32
HEAD_DIM = 64
EPSILON = 1e-05
MASKED = -1e30
HIGHEST = lax.Precision.HIGHEST


def split_up(value, dim, size):
    before, after = (value.shape[:dim], value.shape[dim + 1 :])
    return jnp.moveaxis(value.reshape(*before, size, -1, *after), dim, 0)


def sum_at_owner(value, axis, dim):
    blocks = split_up(value, dim, lax.axis_size(axis))
    arrived = lax.all_to_all(blocks, axis, split_axis=0, concat_axis=0, tiled=True)
    return arrived.astype(jnp.float32).sum(axis=0)


def together(arrays, axis):
    ends = [0]
    for a in arrays:
        ends.append(ends[-1] + a.size)
    so_far = lax.psum(jnp.concatenate([a.ravel() for a in arrays]), axis)
    return tuple((so_far[b:e].reshape(a.shape) for a, b, e in zip(arrays, ends, ends[1:])))


def layer_norm(rows_in, gain, shift):
    row_mean = jnp.mean(rows_in, axis=-1, keepdims=True)
    centered = rows_in - row_mean
    variance = jnp.mean(centered * centered, axis=-1, keepdims=True)
    return centered * lax.rsqrt(variance + EPSILON) * gain + shift


def exact_gelu(values_in):
    return jax.nn.gelu(values_in, approximate=False)


def choose(onehot, tensor_in):
    return jnp.einsum(
        "sa,a...->s...", onehot, tensor_in, preferred_element_type=jnp.float32
    ).astype(jnp.bfloat16)


def spread(onehot, grads_in):
    return jnp.einsum("sa,s...->a...", onehot, grads_in, precision=HIGHEST)


def seq_dot(left_side, right_side):
    return jnp.einsum("slk,skn->sln", left_side, right_side, preferred_element_type=jnp.float32)


def seq_dot_back(left_side, right_side):
    return jnp.einsum("sln,skn->slk", left_side, right_side, preferred_element_type=jnp.float32)


def seq_outer(left_side, right_side):
    return jnp.einsum("slk,sln->skn", left_side, right_side, preferred_element_type=jnp.float32)


def dot_back(left_side, right_side):
    return lax.dot_general(
        left_side, right_side, (((1,), (1,)), ((), ())), preferred_element_type=jnp.float32
    )


def widen_rows(low_rows):
    seq_total = low_rows.shape[0]
    identity = jnp.eye(seq_total, dtype=low_rows.dtype)
    widened = jnp.einsum("slr,st->sltr", low_rows, identity)
    return widened.reshape(seq_total * low_rows.shape[1], seq_total * low_rows.shape[2])


def block_scores(queries, keys_all, slopes, offset, block_rows):
    length = keys_all.shape[0]
    row_ids = offset + jnp.arange(block_rows)
    distance = (row_ids[:, None] - jnp.arange(length)[None, :]).astype(jnp.float32)
    query_block = lax.dynamic_slice_in_dim(queries, offset, block_rows, 0)
    raw_scores = jnp.einsum(
        "qhe,khe->hqk", query_block, keys_all, preferred_element_type=jnp.float32
    )
    scaled = (raw_scores - slopes[:, None, None] * distance[None]) * 0.125
    return (jnp.where(distance[None] >= 0, scaled, MASKED), query_block)


def attend(queries, keys_all, values_all, slopes, block_rows):
    length = queries.shape[0]

    def one_block(block_index):
        scores, _ = block_scores(queries, keys_all, slopes, block_index * block_rows, block_rows)
        row_max = jnp.max(scores, axis=-1, keepdims=True)
        exp_scores = jnp.exp(scores - row_max)
        row_sum = jnp.sum(exp_scores, axis=-1, keepdims=True)
        attn_probs = (exp_scores / row_sum).astype(jnp.bfloat16)
        context = jnp.einsum(
            "hqk,khe->qhe", attn_probs, values_all, preferred_element_type=jnp.float32
        )
        return (context.astype(jnp.bfloat16), (row_max + jnp.log(row_sum))[..., 0])

    context, log_sums = lax.map(one_block, jnp.arange(length // block_rows))
    return (context.reshape(queries.shape), log_sums)


def attend_back(queries, keys_all, values_all, grad_context, log_sums, slopes, block_rows):
    length = queries.shape[0]

    def one_block(running, block_index):
        grad_keys, grad_values = running
        offset = block_index * block_rows
        scores, query_block = block_scores(queries, keys_all, slopes, offset, block_rows)
        grad_block = lax.dynamic_slice_in_dim(grad_context, offset, block_rows, 0)
        attn_probs = jnp.exp(scores - log_sums[block_index][:, :, None])
        grad_probs = jnp.einsum(
            "qhe,khe->hqk", grad_block, values_all, preferred_element_type=jnp.float32
        )
        row_dot = jnp.sum(attn_probs * grad_probs, axis=-1, keepdims=True)
        grad_scores = (attn_probs * (grad_probs - row_dot)).astype(jnp.bfloat16)
        grad_queries = (
            jnp.einsum("hqk,khe->qhe", grad_scores, keys_all, preferred_element_type=jnp.float32)
            * 0.125
        )
        grad_keys = (
            grad_keys
            + jnp.einsum(
                "hqk,qhe->khe", grad_scores, query_block, preferred_element_type=jnp.float32
            )
            * 0.125
        )
        grad_values = grad_values + jnp.einsum(
            "hqk,qhe->khe",
            attn_probs.astype(jnp.bfloat16),
            grad_block,
            preferred_element_type=jnp.float32,
        )
        return ((grad_keys, grad_values), grad_queries)

    zeros_kv = jnp.zeros(keys_all.shape, jnp.float32)
    (grad_keys, grad_values), grad_queries = lax.scan(
        one_block, (zeros_kv, zeros_kv), jnp.arange(length // block_rows)
    )
    return (grad_queries.reshape(queries.shape), grad_keys, grad_values)


def local(
    tokens,
    grad_out,
    adapter_ids,
    first_gain,
    first_shift,
    joined_weight,
    joined_bias,
    dense_weight,
    dense_bias,
    second_gain,
    second_shift,
    up_weight,
    up_bias,
    down_weight,
    down_bias,
    joined_adapt_in,
    joined_adapt_out,
    dense_adapt_in,
    dense_adapt_out,
    up_adapt_in,
    up_adapt_out,
    down_adapt_in,
    down_adapt_out,
):
    local_rows = tokens.shape[0]
    model_width = tokens.shape[1]
    seq_total = adapter_ids.shape[0]
    group_rows = local_rows * lax.axis_size("tp")
    length = group_rows // seq_total
    block_rows = min(512, length)
    set_count = joined_adapt_in.shape[0]
    low_rank = joined_adapt_in.shape[2]
    joined_width = joined_bias.shape[0]
    hidden_width = up_bias.shape[0]
    local_heads = joined_width // (3 * HEAD_DIM)
    head_cols = local_heads * HEAD_DIM
    head_ids = lax.axis_index("tp") * local_heads + jnp.arange(local_heads)
    slopes = jnp.exp2(-8.0 * (head_ids + 1).astype(jnp.float32) / HEADS)
    matches = adapter_ids[:, None] == jnp.arange(set_count)[None, :]
    onehot_low = matches.astype(jnp.bfloat16)
    onehot_high = matches.astype(jnp.float32)
    pick_joined_in = choose(onehot_low, joined_adapt_in)
    pick_joined_out = choose(onehot_low, joined_adapt_out)
    pick_dense_in = choose(onehot_low, dense_adapt_in)
    pick_dense_out = choose(onehot_low, dense_adapt_out)
    pick_up_in = choose(onehot_low, up_adapt_in)
    pick_up_out = choose(onehot_low, up_adapt_out)
    pick_down_in = choose(onehot_low, down_adapt_in)
    pick_down_out = choose(onehot_low, down_adapt_out)
    residual_in = tokens.astype(jnp.float32)
    normed_one = layer_norm(residual_in, first_gain, first_shift).astype(jnp.bfloat16)
    gathered_one = lax.all_gather(normed_one, "tp", axis=0, tiled=True)
    w_joined, w_dense = (
        lax.all_gather(joined_weight, "fsdp", axis=0, tiled=True),
        lax.all_gather(dense_weight, "fsdp", axis=1, tiled=True),
    )
    seq_one = gathered_one.reshape(seq_total, length, model_width)
    low_joined = seq_dot(seq_one, pick_joined_in).astype(jnp.bfloat16)
    joined_cols = jnp.dot(gathered_one, w_joined, preferred_element_type=jnp.float32).reshape(
        seq_total, length, joined_width
    )
    joined_cols = (joined_cols + seq_dot(low_joined, pick_joined_out) + joined_bias).astype(
        jnp.bfloat16
    )
    joined_heads = joined_cols.reshape(seq_total, length, local_heads, 3, HEAD_DIM)
    sequence = 0
    context, log_sums = attend(
        joined_heads[sequence, :, :, 0, :],
        joined_heads[sequence, :, :, 1, :],
        joined_heads[sequence, :, :, 2, :],
        slopes,
        block_rows,
    )
    contexts = [context]
    log_list = [log_sums]
    seq_context = jnp.stack(contexts).reshape(seq_total, length, head_cols)
    context_rows = seq_context.reshape(group_rows, head_cols)
    low_dense = seq_dot(seq_context, pick_dense_in).astype(jnp.bfloat16)
    wide_dense = widen_rows(low_dense)
    stack_dense = pick_dense_out.reshape(seq_total * low_rank, model_width)
    rows_low = wide_dense
    attn_sum = sum_at_owner(
        (
            jnp.dot(context_rows, w_dense, preferred_element_type=jnp.float32)
            + jnp.dot(rows_low, stack_dense, preferred_element_type=jnp.float32)
        ).astype(jnp.bfloat16),
        "tp",
        0,
    )
    residual_mid = residual_in + attn_sum + dense_bias
    normed_two = layer_norm(residual_mid, second_gain, second_shift).astype(jnp.bfloat16)
    gathered_two = lax.all_gather(normed_two, "tp", axis=0, tiled=True)
    w_up, w_down = (
        lax.all_gather(up_weight, "fsdp", axis=0, tiled=True),
        lax.all_gather(down_weight, "fsdp", axis=1, tiled=True),
    )
    seq_two = gathered_two.reshape(seq_total, length, model_width)
    low_up = seq_dot(seq_two, pick_up_in).astype(jnp.bfloat16)
    pre_act = (
        jnp.dot(gathered_two, w_up, preferred_element_type=jnp.float32)
        + seq_dot(low_up, pick_up_out).reshape(group_rows, hidden_width)
        + up_bias
    )
    activated = exact_gelu(pre_act).astype(jnp.bfloat16)
    seq_act = activated.reshape(seq_total, length, hidden_width)
    low_down = seq_dot(seq_act, pick_down_in).astype(jnp.bfloat16)
    wide_down = widen_rows(low_down)
    stack_down = pick_down_out.reshape(seq_total * low_rank, model_width)
    rows_low = wide_down
    mlp_sum = sum_at_owner(
        (
            jnp.dot(activated, w_down, preferred_element_type=jnp.float32)
            + jnp.dot(rows_low, stack_down, preferred_element_type=jnp.float32)
        ).astype(jnp.bfloat16),
        "tp",
        0,
    )
    layer_out = (residual_mid + mlp_sum + down_bias).astype(jnp.bfloat16)
    grad_mlp = lax.all_gather(grad_out, "tp", axis=0, tiled=True)
    back_up, back_down = (w_up, w_down)
    seq_grad_mlp = grad_mlp.reshape(seq_total, length, model_width)
    grad_low_down = seq_dot_back(seq_grad_mlp, pick_down_out).astype(jnp.bfloat16)
    term_down_out = seq_outer(low_down, seq_grad_mlp)
    term_down_in = seq_outer(seq_act, grad_low_down)
    grad_act = dot_back(grad_mlp, back_down) + seq_dot_back(grad_low_down, pick_down_in).reshape(
        group_rows, hidden_width
    )
    _, gelu_pull = jax.vjp(exact_gelu, pre_act)
    grad_pre = gelu_pull(grad_act)[0].astype(jnp.bfloat16)
    seq_grad_pre = grad_pre.reshape(seq_total, length, hidden_width)
    grad_low_up = seq_dot_back(seq_grad_pre, pick_up_out).astype(jnp.bfloat16)
    term_up_out = seq_outer(low_up, seq_grad_pre)
    term_up_in = seq_outer(seq_two, grad_low_up)
    wide_up = widen_rows(grad_low_up)
    stack_up = jnp.swapaxes(pick_up_in, 1, 2).reshape(seq_total * low_rank, model_width)
    rows_grad = grad_pre
    rows_low = wide_up
    grad_norm_two = sum_at_owner(
        (
            dot_back(rows_grad, back_up)
            + jnp.dot(rows_low, stack_up, preferred_element_type=jnp.float32)
        ).astype(jnp.bfloat16),
        "tp",
        0,
    )
    _, norm_pull_two = jax.vjp(
        lambda rows_in: layer_norm(rows_in, second_gain, second_shift), residual_mid
    )
    grad_mid = grad_out.astype(jnp.float32) + norm_pull_two(grad_norm_two)[0]
    grad_attn = lax.all_gather(grad_mid.astype(jnp.bfloat16), "tp", axis=0, tiled=True)
    back_joined, back_dense = (w_joined, w_dense)
    seq_grad_attn = grad_attn.reshape(seq_total, length, model_width)
    grad_low_dense = seq_dot_back(seq_grad_attn, pick_dense_out).astype(jnp.bfloat16)
    term_dense_out = seq_outer(low_dense, seq_grad_attn)
    term_dense_in = seq_outer(seq_context, grad_low_dense)
    grad_context = dot_back(grad_attn, back_dense) + seq_dot_back(
        grad_low_dense, pick_dense_in
    ).reshape(group_rows, head_cols)
    grad_context = grad_context.astype(jnp.bfloat16).reshape(
        seq_total, length, local_heads, HEAD_DIM
    )
    sequence = 0
    grad_query, grad_key, grad_value = attend_back(
        joined_heads[sequence, :, :, 0, :],
        joined_heads[sequence, :, :, 1, :],
        joined_heads[sequence, :, :, 2, :],
        grad_context[sequence],
        log_list[sequence],
        slopes,
        block_rows,
    )
    grad_parts = [jnp.stack((grad_query, grad_key, grad_value), axis=2)]
    grad_joined = (
        jnp.stack(grad_parts).astype(jnp.bfloat16).reshape(seq_total, length, joined_width)
    )
    grad_low_joined = seq_dot_back(grad_joined, pick_joined_out).astype(jnp.bfloat16)
    term_joined_out = seq_outer(low_joined, grad_joined)
    term_joined_in = seq_outer(seq_one, grad_low_joined)
    grad_joined_rows = grad_joined.reshape(group_rows, joined_width)
    wide_joined = widen_rows(grad_low_joined)
    stack_joined = jnp.swapaxes(pick_joined_in, 1, 2).reshape(seq_total * low_rank, model_width)
    rows_grad = grad_joined_rows
    rows_low = wide_joined
    grad_norm_one = sum_at_owner(
        (
            dot_back(rows_grad, back_joined)
            + jnp.dot(rows_low, stack_joined, preferred_element_type=jnp.float32)
        ).astype(jnp.bfloat16),
        "tp",
        0,
    )
    _, norm_pull_one = jax.vjp(
        lambda rows_in: layer_norm(rows_in, first_gain, first_shift), residual_in
    )
    grad_tokens = grad_mid + norm_pull_one(grad_norm_one)[0]
    wide_sums = tuple(
        (
            part.astype(jnp.float32)
            for part in together(
                (
                    spread(onehot_high, term_joined_out).astype(jnp.bfloat16),
                    spread(onehot_high, term_dense_in).astype(jnp.bfloat16),
                    spread(onehot_high, term_up_out).astype(jnp.bfloat16),
                    spread(onehot_high, term_down_in).astype(jnp.bfloat16),
                ),
                "fsdp",
            )
        )
    )
    both_sums = lax.psum(
        (
            spread(onehot_high, term_joined_in),
            spread(onehot_high, term_dense_out),
            spread(onehot_high, term_up_in),
            spread(onehot_high, term_down_out),
        ),
        ("fsdp", "tp"),
    )
    return (
        layer_out,
        grad_tokens,
        both_sums[0],
        wide_sums[0],
        wide_sums[1],
        both_sums[1],
        both_sums[2],
        wide_sums[2],
        wide_sums[3],
        both_sums[3],
    )


def solution(mesh):
    return jax.shard_map(
        local,
        mesh=mesh,
        in_specs=(
            P(("fsdp", "tp"), None),
            P(("fsdp", "tp"), None),
            P("fsdp"),
            P(),
            P(),
            P("fsdp", "tp"),
            P("tp"),
            P("tp", "fsdp"),
            P(),
            P(),
            P(),
            P("fsdp", "tp"),
            P("tp"),
            P("tp", "fsdp"),
            P(),
            P(),
            P(None, None, "tp"),
            P(None, "tp", None),
            P(),
            P(),
            P(None, None, "tp"),
            P(None, "tp", None),
            P(),
        ),
        out_specs=(
            P(("fsdp", "tp"), None),
            P(("fsdp", "tp"), None),
            P(),
            P(None, None, "tp"),
            P(None, "tp", None),
            P(),
            P(),
            P(None, None, "tp"),
            P(None, "tp", None),
            P(),
        ),
        check_vma=False,
    )
```

profile of v0, /device:TPU:1, one launch (start us, length us, event | category | flops | bytes accessed | tf_op | source)
XLA Modules:
  0.0 977.7 jit_solution(4659292120763606901)
XLA Ops:
  19.2 68.6 %all-gather.9.cloned.1.call-done = bf16[1024,2048]{1,0:T(8,128)(2,1)} async-done(((bf16[128,2048]{1,0:T(8,128)(2,1)}), bf16[1024,2048]{1,0:T(8,128)(2,1)}) %all-gather.9.cloned.1.call-update) | async-done | bytes 4194320 | tf_op jit(solution)/shard_map/all_gather | solution.py:200
  91.2 32.7 %all-gather.11.cloned.1.call-done = bf16[2048,768]{1,0:T(8,128)(2,1)} async-done(((bf16[128,768]{1,0:T(8,128)(2,1)}), bf16[2048,768]{1,0:T(8,128)(2,1)}) %all-gather.11.cloned.1.call-update) | async-done | bytes 3145744 | tf_op jit(solution)/shard_map/all_gather | solution.py:202
  123.9 6.4 fusion.96
  131.2 22.1 %while.28 = (s32[]{:T(128)}, bf16[2,512,4,64]{1,3,2,0:T(8,128)(2,1)S(1)}, f32[2,4,512]{2,1,0:T(4,128)S(1)}, s32[2]{0:T(128)S(1)}, bf16[1024,4,64]{0,2,1:T(8,128)...) while((s32[]{:T(128)}, ...), condition=%wide.region_5.6_spmd.clone, body=%wide.region_2.5_spmd.clone.sunk | while | flops 577370624 | bytes 37297388 | solution.py:104
  138.8 3.4 fusion.189
  149.9 3.4 fusion.189
  154.2 5.4 all-gather.13.cloned.1.call-done
  163.4 62.2 %all_to_all.20 = bf16[8,128,2048]{2,1,0:T(8,128)(2,1)S(1)} all-to-all(bf16[8,128,2048]{2,1,0:T(8,128)(2,1)S(1)} %bitcast.233), channel_id=1, replica_groups=mesh['fsdp'=16,'tp'=8] {'tp'}, dimensions={0} | all-to-all | bytes 8388608 | tf_op jit(solution)/shard_map/all_to_all | solution.py:20
  232.0 33.0 %all-gather.21.cloned.1.call-done = bf16[1024,2048]{1,0:T(8,128)(2,1)} async-done(((bf16[128,2048]{1,0:T(8,128)(2,1)}), bf16[1024,2048]{1,0:T(8,128)(2,1)}) %all-gather.21.cloned.1.call-update) | async-done | bytes 4194320 | tf_op jit(solution)/shard_map/all_gather | solution.py:267
  268.3 41.9 %all-gather.19.cloned.1.call-done = bf16[1024,2048]{1,0:T(8,128)(2,1)} async-done(((bf16[1024,128]{1,0:T(8,128)(2,1)}), bf16[1024,2048]{1,0:T(8,128)(2,1)}) %all-gather.19.cloned.1.call-update) | async-done | bytes 4194320 | tf_op jit(solution)/shard_map/all_gather | solution.py:243
  310.2 10.0 %fusion.100 = f32[1024,1024]{1,0:T(8,128)} fusion(bf16[1024,2048]{1,0:T(8,128)(2,1)} %all-gather.21.cloned.1.call-done, bf16[1024,2048]{1,0:T(8,128)(2,1)} %all-gather.19.cloned.1.call-done), kind=kOutput, calls=%fused_computation.187 | convolution fusion | flops 4294967296 | bytes 12582912 | tf_op jit(solution)/shard_map/dot_general | solution.py:66
  320.2 63.6 %all-gather.15.cloned.1.call-done = bf16[1024,2048]{1,0:T(8,128)(2,1)} async-done(((bf16[128,2048]{1,0:T(8,128)(2,1)}), bf16[1024,2048]{1,0:T(8,128)(2,1)}) %all-gather.15.cloned.1.call-update) | async-done | bytes 4194320 | tf_op jit(solution)/shard_map/all_gather | solution.py:240
  387.2 34.3 %all-gather.17.cloned.1.call-done = bf16[2048,1024]{1,0:T(8,128)(2,1)} async-done(((bf16[128,1024]{1,0:T(8,128)(2,1)}), bf16[2048,1024]{1,0:T(8,128)(2,1)}) %all-gather.17.cloned.1.call-update) | async-done | bytes 4194320 | tf_op jit(solution)/shard_map/all_gather | solution.py:242
  421.5 7.9 fusion.98
  429.5 11.2 %multiply_convert_fusion.2 = (bf16[1024,1024]{1,0:T(8,128)(2,1)}, f32[1024,1024]{1,0:T(8,128)S(1)}, f32[1024,1024]{1,0:T(8,128)S(1)}) fusion(f32[1024]{0:T(1024)S(1)} %copy-done.56, f32[1024,1024]{1,0:T(8,128)S(1)} %fusion.98, bf16[1024,16]{0,1:T(8,128)(2,1)S(1)} %convolution_convert_fusion.4, bf16[1,16,1024]{2,0,1:T(2,128)(2,1)S(1)} %fusion.66), kind=kOutput, calls=%fused_computation.60 | convolution fusion | flops 103809024 | bytes 14749696 | tf_op jit(solution)/shard_map/slk,skn->sln/dot_general | solution.py:54
  443.6 4.6 fusion.101
  451.5 6.5 all-to-all-start.2
  460.2 6.9 fusion.99
  470.5 36.2 %all-to-all-done.2 = bf16[8,128,2048]{2,1,0:T(8,128)(2,1)} async-done(((bf16[8,128,2048]{2,1,0:T(8,128)(2,1)}), bf16[8,128,2048]{2,1,0:T(8,128)(2,1)}, u32[]{:S(2)}, u32[]{:S(2)}) %all-to-all-start.2) | async-done | bytes 4194336 | tf_op jit(solution)/shard_map/all_to_all | solution.py:20
  506.8 5.1 all-to-all-start.1
  515.2 45.4 %all-to-all-done.1 = bf16[8,128,2048]{2,1,0:T(8,128)(2,1)} async-done(((bf16[8,128,2048]{2,1,0:T(8,128)(2,1)}), bf16[8,128,2048]{2,1,0:T(8,128)(2,1)}, u32[]{:S(2)}, u32[]{:S(2)}) %all-to-all-start.1) | async-done | bytes 4194336 | tf_op jit(solution)/shard_map/all_to_all | solution.py:20
  576.9 3.7 fusion.109
  581.9 55.0 %all-gather.23.cloned.1.call-done = bf16[1024,2048]{1,0:T(8,128)(2,1)} async-done(((bf16[128,2048]{1,0:T(8,128)(2,1)}), bf16[1024,2048]{1,0:T(8,128)(2,1)}) %all-gather.23.cloned.1.call-update) | async-done | bytes 4194320 | tf_op jit(solution)/shard_map/all_gather | solution.py:298
  636.9 3.5 convolution_convert_fusion.1
  643.7 29.9 %while.29 = (s32[]{:T(128)}, f32[1024,4,64]{0,2,1:T(8,128)S(1)}, f32[1024,4,64]{0,2,1:T(8,128)S(1)}, bf16[2,512,4,64]{1,3,2,0:T(8,128)(2,1)}, s32[2]{0:T(128)S(1...) while((s32[]{:T(128)}, f32[1024,4,64]{0,2,1:T(8,128)S(1)}, ...), condition=%wide.region_15.16_spmd.clone, body=%wide.region_13.15_spmd.clone.sunk | while | flops 1369307648 | bytes 81836928 | solution.py:142
  650.3 3.9 multiply_reduce_fusion.4
  665.0 3.9 multiply_reduce_fusion.4
  679.0 5.4 fusion.103
  687.7 4.6 all-to-all-start.3
  699.3 101.2 %all-reduce.4.cloned.1.call-done = bf16[393216]{0:T(1024)(128)(2,1)} async-done(((bf16[393216]{0:T(1024)(128)(2,1)}), bf16[393216]{0:T(1024)(128)(2,1)}) %all-reduce.4.cloned.1.call-update) | async-done | bytes 786448 | tf_op jit(solution)/shard_map/psum | solution.py:28
  809.3 3.6 copy.47
  818.3 145.4 %all-reduce.6.cloned.1.call-done = (f32[8,2048,16]{1,2,0:T(8,128)}, f32[8,16,2048]{2,1,0:T(8,128)}, f32[8,2048,16]{1,2,0:T(8,128)}, f32[8,16,2048]{2,1,0:T(8,128)}) async-done(((f32[8,2048,16]{1,2,0:T(8,128)}, f32[8,16,2048]{2,1,0:T(8,128)}, f32[8,2048,16]{1,2,0:T(8,128)}, f32[8,16,2048]{2,1,0:T(8,128)}), (f32[8,2048,16]{1,2,0:T(8,128)}, f32[8,16,2048]{2,1,0:T(8,128)}, f32[8,2048,16]{1,2,0:T(8,128)}, ...) | async-done | bytes 4194320 | tf_op jit(solution)/shard_map/psum | solution.py:358
  (279 shorter events, 135.5 us)
Async XLA Ops:
  7.2 10.6 %copy-start = (bf16[8,2048,16]{1,2,0:T(8,128)(2,1)S(1)}, bf16[8,2048,16]{1,2,0:T(8,128)(2,1)}, u32[]{:S(2)}) copy-start(bf16[8,2048,16]{1,2,0:T(8,128)(2,1)} %param.42) | copy-start | bytes 1572868
  7.2 11.3 %copy-start.38 = (bf16[8,16,768]{2,1,0:T(8,128)(2,1)S(1)}, bf16[8,16,768]{2,1,0:T(8,128)(2,1)}, u32[]{:S(2)}) copy-start(bf16[8,16,768]{2,1,0:T(8,128)(2,1)} %param.43) | copy-start | bytes 589828
  7.2 11.5 %copy-start.24 = (bf16[8,16,2048]{2,1,0:T(8,128)(2,1)S(1)}, bf16[8,16,2048]{2,1,0:T(8,128)(2,1)}, u32[]{:S(2)}) copy-start(bf16[8,16,2048]{2,1,0:T(8,128)(2,1)} %param.45) | copy-start | bytes 1572868
  7.2 80.6 %all-gather.9.cloned.1.call-start = ((), (), s32[]{:S(2)}) async-start(), calls=%async_computation.4 | async-start | bytes 4718592 | tf_op jit(solution)/shard_map/all_gather | solution.py:200
  13.3 110.7 %all-gather.11.cloned.1.call-start = ((), (), s32[]{:S(2)}) async-start(), calls=%async_computation.5 | async-start | bytes 3342336 | tf_op jit(solution)/shard_map/all_gather | solution.py:202
  14.0 145.6 %all-gather.13.cloned.1.call-start = ((), (), s32[]{:S(2)}) async-start(), calls=%async_computation.6 | async-start | bytes 1114112 | tf_op jit(solution)/shard_map/all_gather | solution.py:203
  14.7 250.2 %all-gather.21.cloned.1.call-start = ((), (), s32[]{:S(2)}) async-start(), calls=%async_computation.10 | async-start | bytes 4718592 | tf_op jit(solution)/shard_map/all_gather | solution.py:267
  15.3 294.9 %all-gather.19.cloned.1.call-start = ((), (), s32[]{:S(2)}) async-start(), calls=%async_computation.9 | async-start | bytes 4456448 | tf_op jit(solution)/shard_map/all_gather | solution.py:243
  15.9 367.9 %all-gather.15.cloned.1.call-start = ((), (), s32[]{:S(2)}) async-start(), calls=%async_computation.7 | async-start | bytes 4718592 | tf_op jit(solution)/shard_map/all_gather | solution.py:240
  18.5 72.6 %copy-start.14 = (bf16[1,2048,16]{2,1,0:T(8,128)(2,1)}, bf16[1,2048,16]{2,1,0:T(8,128)(2,1)S(1)}, u32[]{:S(2)}) copy-start(bf16[1,2048,16]{2,1,0:T(8,128)(2,1)S(1)} %copy.49) | copy-start | bytes 196612
  18.7 111.6 %copy-start.36 = (bf16[1,16,768]{2,0,1:T(2,128)(2,1)}, bf16[1,16,768]{2,0,1:T(2,128)(2,1)S(1)}, u32[]{:S(2)}) copy-start(bf16[1,16,768]{2,0,1:T(2,128)(2,1)S(1)} %fusion.68) | copy-start | bytes 73732
  19.2 142.9 %copy-start.28 = (bf16[1,16,2048]{2,0,1:T(2,128)(2,1)}, bf16[1,16,2048]{2,0,1:T(2,128)(2,1)S(1)}, u32[]{:S(2)}) copy-start(bf16[1,16,2048]{2,0,1:T(2,128)(2,1)S(1)} %fusion.60) | copy-start | bytes 196612
  91.1 39.2 %copy-start.30 = (bf16[1024,16]{0,1:T(8,128)(2,1)}, bf16[1024,16]{0,1:T(8,128)(2,1)S(1)}, u32[]{:S(2)}) copy-start(bf16[1024,16]{0,1:T(8,128)(2,1)S(1)} %convolution_convert_fusion.5) | copy-start | bytes 98308
  91.1 39.2 %copy-start.50 = (f32[768]{0:T(1024)S(1)}, f32[768]{0:T(1024)}, u32[]{:S(2)}) copy-start(f32[768]{0:T(1024)} %param.33) | copy-start | bytes 9220
  153.3 8.8 copy-start.8
  153.9 8.2 copy-start.11
  154.2 8.0 copy-start.32
  228.3 193.3 %all-gather.17.cloned.1.call-start = ((), (), s32[]{:S(2)}) async-start(), calls=%async_computation.8 | async-start | bytes 4456448 | tf_op jit(solution)/shard_map/all_gather | solution.py:242
  387.2 42.3 %copy-start.56 = (f32[1024]{0:T(1024)S(1)}, f32[1024]{0:T(1024)}, u32[]{:S(2)}) copy-start(f32[1024]{0:T(1024)} %param.39) | copy-start | bytes 12292
  429.5 11.2 %copy-start.57 = (f32[1024,1024]{1,0:T(8,128)S(1)}, f32[1024,1024]{1,0:T(8,128)}, u32[]{:S(2)}) copy-start(f32[1024,1024]{1,0:T(8,128)} %fusion.100) | copy-start | bytes 12582916
  451.5 55.3 %all-to-all-start.2 = ((bf16[8,128,2048]{2,1,0:T(8,128)(2,1)}), bf16[8,128,2048]{2,1,0:T(8,128)(2,1)}, u32[]{:S(2)}, u32[]{:S(2)}) async-start(bf16[8,128,2048]{2,1,0:T(8,128)(2,1)} %bitcast.232), calls=%async_computation.2 | async-start | bytes 8388608 | tf_op jit(solution)/shard_map/all_to_all | solution.py:20
  506.8 53.8 %all-to-all-start.1 = ((bf16[8,128,2048]{2,1,0:T(8,128)(2,1)}), bf16[8,128,2048]{2,1,0:T(8,128)(2,1)}, u32[]{:S(2)}, u32[]{:S(2)}) async-start(bf16[8,128,2048]{2,1,0:T(8,128)(2,1)} %bitcast.231), calls=%async_computation.1 | async-start | bytes 8388608 | tf_op jit(solution)/shard_map/all_to_all | solution.py:20
  511.8 125.0 %all-gather.23.cloned.1.call-start = ((), (), s32[]{:S(2)}) async-start(), calls=%async_computation.11 | async-start | bytes 4718592 | tf_op jit(solution)/shard_map/all_gather | solution.py:298
  514.9 48.7 %copy-start.47 = (f32[2048]{0:T(1024)S(1)}, f32[2048]{0:T(1024)}, u32[]{:S(2)}) copy-start(f32[2048]{0:T(1024)} %param.41) | copy-start | bytes 24580
  566.8 233.7 %all-reduce.4.cloned.1.call-start = ((), (), s32[]{:S(2)}) async-start(), calls=%async_computation.12 | async-start | bytes 1572864 | tf_op jit(solution)/shard_map/psum | solution.py:28
  687.7 125.2 %all-to-all-start.3 = ((bf16[8,128,2048]{2,1,0:T(8,128)(2,1)}), bf16[8,128,2048]{2,1,0:T(8,128)(2,1)}, u32[]{:S(2)}, u32[]{:S(2)}) async-start(bf16[8,128,2048]{2,1,0:T(8,128)(2,1)} %bitcast.230), calls=%async_computation.3 | async-start | bytes 8388608 | tf_op jit(solution)/shard_map/all_to_all | solution.py:20
  692.3 271.4 %all-reduce.6.cloned.1.call-start = ((), (), s32[]{:S(2)}) async-start(), calls=%async_computation.13 | async-start | bytes 8388608 | tf_op jit(solution)/shard_map/psum | solution.py:358
  809.3 6.7 copy-start.4
  809.3 6.7 copy-start.39
  809.3 6.7 copy-start.44
  963.7 5.7 copy-start.19
  963.7 6.7 copy-start.1
  (42 other events, 111.3 us)
Sparse Core Ops, SparseCore 0:
  13.4 74.3 all-gather.8
  89.5 34.3 all-gather.10
  125.5 33.9 all-gather.12
  161.8 103.1 all-gather.20
  266.4 43.7 all-gather.18
  313.0 70.7 all-gather.14
  385.6 35.9 all-gather.16
  566.9 69.9 all-gather.22
  679.1 121.3 all-reduce.3
  807.4 156.1 all-reduce.5
where the time goes:
time: 982 us; the launch traced here: 978 us
  waiting for transfers between devices  666 us (68%)
  matrix products  139 us (14%)
  blocking collectives  62.2 us (6%)
  other arithmetic  40.9 us (4%)
  local copies, waits for them, and re-layouts  29.7 us (3%)
  starting transfers between devices  16.5 us (2%)
  between operations  16.2 us (2%)
    psum x1, waiting for transfers between devices, local(): lax.psum((spread(onehot_high, term_joined_in), spread(onehot_high, term_d...  145 us
    psum x1, waiting for transfers between devices, together(): so_far = lax.psum(jnp.concatenate([a.ravel() for a in arrays]), axis)  101 us
    all_to_all x3, waiting for transfers between devices, sum_at_owner(): lax.all_to_all(blocks, axis, split_axis=0, concat_axis=0, tiled=True)  81.6 us
    all_gather x1, waiting for transfers between devices, local(): gathered_one = lax.all_gather(normed_one, 'tp', axis=0, tiled=True)  68.6 us
    all_gather x1, waiting for transfers between devices, local(): gathered_two = lax.all_gather(normed_two, 'tp', axis=0, tiled=True)  63.6 us
    all_to_all x1, blocking collectives, sum_at_owner(): lax.all_to_all(blocks, axis, split_axis=0, concat_axis=0, tiled=True)  62.2 us
    all_gather x1, waiting for transfers between devices, local(): lax.all_gather(grad_mid.astype(jnp.bfloat16), 'tp', axis=0, tiled=True)  55 us
    all_gather x1, waiting for transfers between devices, local(): lax.all_gather(down_weight, 'fsdp', axis=1, tiled=True)  41.9 us
  transfers between devices with their start and end apart: 13, of which 12 were waited for; matrix products, arithmetic and copies ran while one was open for 13% of the time, Pallas kernels for 0%

commit v1 on v0

--- a/solution.py
+++ b/solution.py
@@ -355,15 +355,14 @@
             )
         )
     )
-    both_sums = lax.psum(
-        (
-            spread(onehot_high, term_joined_in),
-            spread(onehot_high, term_dense_out),
-            spread(onehot_high, term_up_in),
-            spread(onehot_high, term_down_out),
-        ),
-        ("fsdp", "tp"),
-    )
+    both_sums = (
+        spread(onehot_high, term_joined_in),
+        spread(onehot_high, term_dense_out),
+        spread(onehot_high, term_up_in),
+        spread(onehot_high, term_down_out),
+    )
+    for mesh_axis in ("fsdp", "tp"):
+        both_sums = lax.psum(both_sums, mesh_axis)
     return (
         layer_out,
         grad_tokens,

time: 982 us -> 1070 us (1.090)
  waiting for transfers between devices: 666 us -> 751 us
    psum x1 -> x2, waiting for transfers between devices: 145 us -> 232 us  [local(): both_sums = lax.psum(both_sums, mesh_axis)]
  transfers between devices with their start and end apart: 13 -> 14, of which waited for: 12 -> 13; matrix products, arithmetic and copies ran while one was open for 13% -> 12% of each run, Pallas kernels for 0% -> 0%
where the time goes in v1:
time: 1070 us; the launch traced here: 1060 us
  waiting for transfers between devices  751 us (70%)
  matrix products  139 us (13%)
  blocking collectives  62.2 us (6%)
  other arithmetic  40.9 us (4%)
  local copies, waits for them, and re-layouts  28.5 us (3%)
  starting transfers between devices  16.8 us (2%)
  between operations  15.9 us (1%)
    psum x2, waiting for transfers between devices, local(): both_sums = lax.psum(both_sums, mesh_axis)  232 us
    psum x1, waiting for transfers between devices, together(): so_far = lax.psum(jnp.concatenate([a.ravel() for a in arrays]), axis)  100 us
    all_to_all x3, waiting for transfers between devices, sum_at_owner(): lax.all_to_all(blocks, axis, split_axis=0, concat_axis=0, tiled=True)  81.6 us
    all_gather x1, waiting for transfers between devices, local(): gathered_one = lax.all_gather(normed_one, 'tp', axis=0, tiled=True)  68.5 us
    all_gather x1, waiting for transfers between devices, local(): gathered_two = lax.all_gather(normed_two, 'tp', axis=0, tiled=True)  63.6 us
    all_to_all x1, blocking collectives, sum_at_owner(): lax.all_to_all(blocks, axis, split_axis=0, concat_axis=0, tiled=True)  62.2 us
    all_gather x1, waiting for transfers between devices, local(): lax.all_gather(grad_mid.astype(jnp.bfloat16), 'tp', axis=0, tiled=True)  55 us
    all_gather x1, waiting for transfers between devices, local(): lax.all_gather(down_weight, 'fsdp', axis=1, tiled=True)  41.9 us
  transfers between devices with their start and end apart: 14, of which 13 were waited for; matrix products, arithmetic and copies ran while one was open for 12% of the time, Pallas kernels for 0%

profile of v1, /device:TPU:1, one launch (start us, length us, event | category | flops | bytes accessed | tf_op | source)
XLA Modules:
  0.0 1061.4 jit_solution(16100968086034289109)
XLA Ops:
  18.2 68.5 %all-gather.9.cloned.1.call-done = bf16[1024,2048]{1,0:T(8,128)(2,1)} async-done(((bf16[128,2048]{1,0:T(8,128)(2,1)}), bf16[1024,2048]{1,0:T(8,128)(2,1)}) %all-gather.9.cloned.1.call-update) | async-done | bytes 4194320 | tf_op jit(solution)/shard_map/all_gather | solution.py:200
  90.1 32.7 %all-gather.11.cloned.1.call-done = bf16[2048,768]{1,0:T(8,128)(2,1)} async-done(((bf16[128,768]{1,0:T(8,128)(2,1)}), bf16[2048,768]{1,0:T(8,128)(2,1)}) %all-gather.11.cloned.1.call-update) | async-done | bytes 3145744 | tf_op jit(solution)/shard_map/all_gather | solution.py:202
  122.9 6.4 fusion.96
  130.1 22.1 %while.28 = (s32[]{:T(128)}, bf16[2,512,4,64]{1,3,2,0:T(8,128)(2,1)S(1)}, f32[2,4,512]{2,1,0:T(4,128)S(1)}, s32[2]{0:T(128)S(1)}, bf16[1024,4,64]{0,2,1:T(8,128)...) while((s32[]{:T(128)}, ...), condition=%wide.region_5.6_spmd.clone, body=%wide.region_2.5_spmd.clone.sunk | while | flops 577370624 | bytes 37297388 | solution.py:104
  148.8 3.4 fusion.189
  153.1 5.4 all-gather.13.cloned.1.call-done
  162.4 62.2 %all_to_all.20 = bf16[8,128,2048]{2,1,0:T(8,128)(2,1)S(1)} all-to-all(bf16[8,128,2048]{2,1,0:T(8,128)(2,1)S(1)} %bitcast.233), channel_id=1, replica_groups=mesh['fsdp'=16,'tp'=8] {'tp'}, dimensions={0} | all-to-all | bytes 8388608 | tf_op jit(solution)/shard_map/all_to_all | solution.py:20
  231.0 32.9 %all-gather.21.cloned.1.call-done = bf16[1024,2048]{1,0:T(8,128)(2,1)} async-done(((bf16[128,2048]{1,0:T(8,128)(2,1)}), bf16[1024,2048]{1,0:T(8,128)(2,1)}) %all-gather.21.cloned.1.call-update) | async-done | bytes 4194320 | tf_op jit(solution)/shard_map/all_gather | solution.py:267
  267.3 41.9 %all-gather.19.cloned.1.call-done = bf16[1024,2048]{1,0:T(8,128)(2,1)} async-done(((bf16[1024,128]{1,0:T(8,128)(2,1)}), bf16[1024,2048]{1,0:T(8,128)(2,1)}) %all-gather.19.cloned.1.call-update) | async-done | bytes 4194320 | tf_op jit(solution)/shard_map/all_gather | solution.py:243
  309.2 10.0 fusion.100
  319.2 63.6 %all-gather.15.cloned.1.call-done = bf16[1024,2048]{1,0:T(8,128)(2,1)} async-done(((bf16[128,2048]{1,0:T(8,128)(2,1)}), bf16[1024,2048]{1,0:T(8,128)(2,1)}) %all-gather.15.cloned.1.call-update) | async-done | bytes 4194320 | tf_op jit(solution)/shard_map/all_gather | solution.py:240
  386.2 34.3 %all-gather.17.cloned.1.call-done = bf16[2048,1024]{1,0:T(8,128)(2,1)} async-done(((bf16[128,1024]{1,0:T(8,128)(2,1)}), bf16[2048,1024]{1,0:T(8,128)(2,1)}) %all-gather.17.cloned.1.call-update) | async-done | bytes 4194320 | tf_op jit(solution)/shard_map/all_gather | solution.py:242
  420.5 8.0 fusion.98
  428.4 11.2 %multiply_convert_fusion.2 = (bf16[1024,1024]{1,0:T(8,128)(2,1)}, f32[1024,1024]{1,0:T(8,128)S(1)}, f32[1024,1024]{1,0:T(8,128)S(1)}) fusion(f32[1024]{0:T(1024)S(1)} %copy-done.56, f32[1024,1024]{1,0:T(8,128)S(1)} %fusion.98, bf16[1024,16]{0,1:T(8,128)(2,1)S(1)} %convolution_convert_fusion.4, bf16[1,16,1024]{2,0,1:T(2,128)(2,1)S(1)} %fusion.66), kind=kOutput, calls=%fused_computation.60 | convolution fusion | flops 103809024 | bytes 14749696 | tf_op jit(solution)/shard_map/slk,skn->sln/dot_general | solution.py:54
  442.6 4.6 fusion.101
  450.4 6.5 all-to-all-start.2
  459.2 6.9 fusion.99
  469.5 36.2 %all-to-all-done.2 = bf16[8,128,2048]{2,1,0:T(8,128)(2,1)} async-done(((bf16[8,128,2048]{2,1,0:T(8,128)(2,1)}), bf16[8,128,2048]{2,1,0:T(8,128)(2,1)}, u32[]{:S(2)}, u32[]{:S(2)}) %all-to-all-start.2) | async-done | bytes 4194336 | tf_op jit(solution)/shard_map/all_to_all | solution.py:20
  505.7 5.1 all-to-all-start.1
  514.2 45.4 %all-to-all-done.1 = bf16[8,128,2048]{2,1,0:T(8,128)(2,1)} async-done(((bf16[8,128,2048]{2,1,0:T(8,128)(2,1)}), bf16[8,128,2048]{2,1,0:T(8,128)(2,1)}, u32[]{:S(2)}, u32[]{:S(2)}) %all-to-all-start.1) | async-done | bytes 4194336 | tf_op jit(solution)/shard_map/all_to_all | solution.py:20
  575.9 3.7 fusion.109
  580.9 55.0 %all-gather.23.cloned.1.call-done = bf16[1024,2048]{1,0:T(8,128)(2,1)} async-done(((bf16[128,2048]{1,0:T(8,128)(2,1)}), bf16[1024,2048]{1,0:T(8,128)(2,1)}) %all-gather.23.cloned.1.call-update) | async-done | bytes 4194320 | tf_op jit(solution)/shard_map/all_gather | solution.py:298
  635.9 3.5 convolution_convert_fusion.1
  642.7 29.7 %while.29 = (s32[]{:T(128)}, f32[1024,4,64]{0,2,1:T(8,128)S(1)}, f32[1024,4,64]{0,2,1:T(8,128)S(1)}, bf16[2,512,4,64]{1,3,2,0:T(8,128)(2,1)}, s32[2]{0:T(128)S(1...) while((s32[]{:T(128)}, f32[1024,4,64]{0,2,1:T(8,128)S(1)}, ...), condition=%wide.region_15.16_spmd.clone, body=%wide.region_13.15_spmd.clone.sunk | while | flops 1369307648 | bytes 81836928 | solution.py:142
  649.2 3.9 multiply_reduce_fusion.4
  663.9 3.9 multiply_reduce_fusion.4
  685.0 5.4 fusion.103
  693.7 4.6 all-to-all-start.3
  698.4 100.2 %all-reduce.6.cloned.1.call-done = bf16[393216]{0:T(1024)(128)(2,1)} async-done(((bf16[393216]{0:T(1024)(128)(2,1)}), bf16[393216]{0:T(1024)(128)(2,1)}) %all-reduce.6.cloned.1.call-update) | async-done | bytes 786448 | tf_op jit(solution)/shard_map/psum | solution.py:28
  799.6 132.5 %all-reduce.8.cloned.1.call-done = (f32[8,2048,16]{1,2,0:T(8,128)}, f32[8,16,2048]{2,1,0:T(8,128)}, f32[8,2048,16]{1,2,0:T(8,128)}, f32[8,16,2048]{2,1,0:T(8,128)}) async-done(((f32[8,2048,16]{1,2,0:T(8,128)}, f32[8,16,2048]{2,1,0:T(8,128)}, f32[8,2048,16]{1,2,0:T(8,128)}, f32[8,16,2048]{2,1,0:T(8,128)}), (f32[8,2048,16]{1,2,0:T(8,128)}, f32[8,16,2048]{2,1,0:T(8,128)}, f32[8,2048,16]{1,2,0:T(8,128)}, ...) | async-done | bytes 4194320 | tf_op jit(solution)/shard_map/psum | solution.py:365
  939.6 3.6 copy.47
  948.6 99.1 %all-reduce.10.cloned.1.call-done = (f32[8,2048,16]{1,2,0:T(8,128)}, f32[8,16,2048]{2,1,0:T(8,128)}, f32[8,2048,16]{1,2,0:T(8,128)}, f32[8,16,2048]{2,1,0:T(8,128)}) async-done(((f32[8,2048,16]{1,2,0:T(8,128)}, f32[8,16,2048]{2,1,0:T(8,128)}, f32[8,2048,16]{1,2,0:T(8,128)}, f32[8,16,2048]{2,1,0:T(8,128)}), (f32[8,2048,16]{1,2,0:T(8,128)}, f32[8,16,2048]{2,1,0:T(8,128)}, f32[8,2048,16]{1,2,0:T(8,128)}, ...) | async-done | bytes 4194320 | tf_op jit(solution)/shard_map/psum | solution.py:365
  (282 shorter events, 137.9 us)
Async XLA Ops:
  7.2 9.5 copy-start
  7.2 10.3 copy-start.38
  7.2 10.5 copy-start.24
  7.2 79.5 %all-gather.9.cloned.1.call-start = ((), (), s32[]{:S(2)}) async-start(), calls=%async_computation.4 | async-start | bytes 4718592 | tf_op jit(solution)/shard_map/all_gather | solution.py:200
  8.5 8.1 copy-start.43
  9.9 6.8 copy-start.53
  9.9 6.8 copy-start.48
  12.2 110.7 %all-gather.11.cloned.1.call-start = ((), (), s32[]{:S(2)}) async-start(), calls=%async_computation.5 | async-start | bytes 3342336 | tf_op jit(solution)/shard_map/all_gather | solution.py:202
  12.9 145.6 %all-gather.13.cloned.1.call-start = ((), (), s32[]{:S(2)}) async-start(), calls=%async_computation.6 | async-start | bytes 1114112 | tf_op jit(solution)/shard_map/all_gather | solution.py:203
  13.7 250.2 %all-gather.21.cloned.1.call-start = ((), (), s32[]{:S(2)}) async-start(), calls=%async_computation.10 | async-start | bytes 4718592 | tf_op jit(solution)/shard_map/all_gather | solution.py:267
  14.3 294.9 %all-gather.19.cloned.1.call-start = ((), (), s32[]{:S(2)}) async-start(), calls=%async_computation.9 | async-start | bytes 4456448 | tf_op jit(solution)/shard_map/all_gather | solution.py:243
  14.8 368.0 %all-gather.15.cloned.1.call-start = ((), (), s32[]{:S(2)}) async-start(), calls=%async_computation.7 | async-start | bytes 4718592 | tf_op jit(solution)/shard_map/all_gather | solution.py:240
  17.5 72.6 %copy-start.14 = (bf16[1,2048,16]{2,1,0:T(8,128)(2,1)}, bf16[1,2048,16]{2,1,0:T(8,128)(2,1)S(1)}, u32[]{:S(2)}) copy-start(bf16[1,2048,16]{2,1,0:T(8,128)(2,1)S(1)} %copy.49) | copy-start | bytes 196612
  17.7 111.6 %copy-start.36 = (bf16[1,16,768]{2,0,1:T(2,128)(2,1)}, bf16[1,16,768]{2,0,1:T(2,128)(2,1)S(1)}, u32[]{:S(2)}) copy-start(bf16[1,16,768]{2,0,1:T(2,128)(2,1)S(1)} %fusion.68) | copy-start | bytes 73732
  18.2 142.9 %copy-start.28 = (bf16[1,16,2048]{2,0,1:T(2,128)(2,1)}, bf16[1,16,2048]{2,0,1:T(2,128)(2,1)S(1)}, u32[]{:S(2)}) copy-start(bf16[1,16,2048]{2,0,1:T(2,128)(2,1)S(1)} %fusion.60) | copy-start | bytes 196612
  90.1 39.2 %copy-start.30 = (bf16[1024,16]{0,1:T(8,128)(2,1)}, bf16[1024,16]{0,1:T(8,128)(2,1)S(1)}, u32[]{:S(2)}) copy-start(bf16[1024,16]{0,1:T(8,128)(2,1)S(1)} %convolution_convert_fusion.5) | copy-start | bytes 98308
  90.1 39.2 %copy-start.50 = (f32[768]{0:T(1024)S(1)}, f32[768]{0:T(1024)}, u32[]{:S(2)}) copy-start(f32[768]{0:T(1024)} %param.33) | copy-start | bytes 9220
  152.2 8.8 copy-start.8
  152.9 8.2 copy-start.11
  153.1 8.0 copy-start.32
  227.2 193.2 %all-gather.17.cloned.1.call-start = ((), (), s32[]{:S(2)}) async-start(), calls=%async_computation.8 | async-start | bytes 4456448 | tf_op jit(solution)/shard_map/all_gather | solution.py:242
  386.2 42.3 %copy-start.56 = (f32[1024]{0:T(1024)S(1)}, f32[1024]{0:T(1024)}, u32[]{:S(2)}) copy-start(f32[1024]{0:T(1024)} %param.39) | copy-start | bytes 12292
  428.4 11.2 %copy-start.57 = (f32[1024,1024]{1,0:T(8,128)S(1)}, f32[1024,1024]{1,0:T(8,128)}, u32[]{:S(2)}) copy-start(f32[1024,1024]{1,0:T(8,128)} %fusion.100) | copy-start | bytes 12582916
  450.4 55.3 %all-to-all-start.2 = ((bf16[8,128,2048]{2,1,0:T(8,128)(2,1)}), bf16[8,128,2048]{2,1,0:T(8,128)(2,1)}, u32[]{:S(2)}, u32[]{:S(2)}) async-start(bf16[8,128,2048]{2,1,0:T(8,128)(2,1)} %bitcast.232), calls=%async_computation.2 | async-start | bytes 8388608 | tf_op jit(solution)/shard_map/all_to_all | solution.py:20
  505.7 53.8 %all-to-all-start.1 = ((bf16[8,128,2048]{2,1,0:T(8,128)(2,1)}), bf16[8,128,2048]{2,1,0:T(8,128)(2,1)}, u32[]{:S(2)}, u32[]{:S(2)}) async-start(bf16[8,128,2048]{2,1,0:T(8,128)(2,1)} %bitcast.231), calls=%async_computation.1 | async-start | bytes 8388608 | tf_op jit(solution)/shard_map/all_to_all | solution.py:20
  510.8 125.0 %all-gather.23.cloned.1.call-start = ((), (), s32[]{:S(2)}) async-start(), calls=%async_computation.11 | async-start | bytes 4718592 | tf_op jit(solution)/shard_map/all_gather | solution.py:298
  513.9 48.7 %copy-start.47 = (f32[2048]{0:T(1024)S(1)}, f32[2048]{0:T(1024)}, u32[]{:S(2)}) copy-start(f32[2048]{0:T(1024)} %param.41) | copy-start | bytes 24580
  565.8 232.8 %all-reduce.6.cloned.1.call-start = ((), (), s32[]{:S(2)}) async-start(), calls=%async_computation.12 | async-start | bytes 1572864 | tf_op jit(solution)/shard_map/psum | solution.py:28
  677.8 254.4 %all-reduce.8.cloned.1.call-start = ((), (), s32[]{:S(2)}) async-start(), calls=%async_computation.13 | async-start | bytes 8388608 | tf_op jit(solution)/shard_map/psum | solution.py:365
  693.7 249.5 %all-to-all-start.3 = ((bf16[8,128,2048]{2,1,0:T(8,128)(2,1)}), bf16[8,128,2048]{2,1,0:T(8,128)(2,1)}, u32[]{:S(2)}, u32[]{:S(2)}) async-start(bf16[8,128,2048]{2,1,0:T(8,128)(2,1)} %bitcast.230), calls=%async_computation.3 | async-start | bytes 8388608 | tf_op jit(solution)/shard_map/all_to_all | solution.py:20
  698.3 349.4 %all-reduce.10.cloned.1.call-start = ((), (), s32[]{:S(2)}) async-start(), calls=%async_computation.14 | async-start | bytes 8388608 | tf_op jit(solution)/shard_map/psum | solution.py:365
  939.6 6.7 copy-start.44
  (43 other events, 137.5 us)
Sparse Core Ops, SparseCore 0:
  12.3 74.3 all-gather.8
  88.4 34.3 all-gather.10
  124.5 33.9 all-gather.12
  160.7 103.1 all-gather.20
  265.4 43.7 all-gather.18
  312.0 70.7 all-gather.14
  384.5 35.9 all-gather.16
  565.9 69.9 all-gather.22
  677.9 120.6 all-reduce.5
  801.9 130.1 all-reduce.7
  935.1 112.5 all-reduce.9
